TPU v7x, 128 devices: a whole 4x4x4 slice. The times are simulated.
128 devices in a mesh: row: 16 (over x_lo, y, core), col: 8 (over x_hi, z).
Axes of the slice: x: 4 (x_hi: 2, x_lo: 2; x = x_hi * 2 + x_lo), y: 4, z: 4, core: 2. Of those that a mesh axis runs over, the one named last changes fastest.
Arguments:
- nodes: bfloat16 [32768, 256], P(('row', 'col')), may hold values from -6 to 6
- weight: bfloat16 [256, 256], replicated, may hold values from -0.375 to 0.375
- adjacency: bfloat16 [32768, 32768], P('row', 'col'), may hold values from -0.046875 to 0.046875
- history: bfloat16 [131072, 256], P(('row', 'col')), may hold values from -6 to 6
- pull_owner: int32 [4096, 1], P(('row', 'col')), may hold values from 0 to 15; in each aligned block of 32 rows (0 to 31, 32 to 63, ...) at most 4 rows name the same one
- pull_slot: int32 [4096], P(('row', 'col')), may hold values from 0 to 7
- pull_target: int32 [4096], P(('row', 'col')), may hold values from 0 to 15
- hist_tiles: bfloat16 [4096, 128, 128], P(('row', 'col')), may hold values from -0.375 to 0.375
- cotangent: bfloat16 [32768, 256], P(('row', 'col')), may hold values from -6 to 6
Outputs:
- activated: bfloat16 [32768, 256], P(('row', 'col'))
- grad_nodes: bfloat16 [32768, 256], P(('row', 'col'))
- grad_weight: float32 [256, 256], replicated
Inputs may be any that keep to these rules, and one draw needn't show every extreme that they name: `pull_owner`: among the 32 pulls of one device no owner is named more than 4 times, a bound that some block reaches.
All inputs are finite; a program needn't handle non-finite values.
Results may differ from a plain program's by a relative error of at most 0.029.
Values may be sent and summed in bfloat16 or wider, within the bound.
A program may use at most 128 MiB of HBM per device.

v0:
```python
import math
import jax
import jax.numpy as jnp
from jax import lax
from jax.sharding import PartitionSpec as P

HID = 256
BLK = 128


def local(
    nodes, weight, adjacency, history, pull_owner, pull_slot, pull_target, hist_tiles, cotangent
):
    projected = jnp.dot(nodes, weight, preferred_element_type=jnp.float32).astype(jnp.bfloat16)
    gathered = lax.all_gather(projected, "row", axis=0, tiled=True)
    owners = pull_owner[:, 0]
    blocks = history.reshape(-1, BLK, HID)
    everything = lax.all_gather(blocks, "row", axis=0, tiled=True)
    pulled = everything[owners * blocks.shape[0] + pull_slot]
    products = jnp.einsum("kab,kbf->kaf", hist_tiles, pulled, preferred_element_type=jnp.float32)
    row_count = adjacency.shape[0] // BLK
    placing = (pull_target[None, :] == jnp.arange(row_count, dtype=jnp.int32)[:, None]).astype(
        jnp.float32
    )
    history_term = jnp.einsum(
        "jk,kaf->jaf", placing, products, precision=lax.Precision.HIGHEST
    ).reshape(-1, HID)
    in_batch = jnp.dot(adjacency, gathered, preferred_element_type=jnp.float32)
    mixed = lax.psum_scatter(
        (in_batch + history_term).astype(jnp.bfloat16), "col", scatter_dimension=0, tiled=True
    ).astype(jnp.float32)
    activated = jax.nn.silu(mixed).astype(jnp.bfloat16)
    sigmoid_z = jax.nn.sigmoid(mixed)
    grad_pre = (
        cotangent.astype(jnp.float32) * sigmoid_z * (1.0 + mixed * (1.0 - sigmoid_z))
    ).astype(jnp.bfloat16)
    grad_panel = lax.all_gather(grad_pre, "col", axis=0, tiled=True)
    grad_proj = lax.psum_scatter(
        lax.dot_general(
            adjacency, grad_panel, (((0,), (0,)), ((), ())), preferred_element_type=jnp.float32
        ).astype(jnp.bfloat16),
        "row",
        scatter_dimension=0,
        tiled=True,
    )
    grad_nodes = jnp.dot(grad_proj, weight.T, preferred_element_type=jnp.float32).astype(
        jnp.bfloat16
    )
    partial_grad = lax.dot_general(
        nodes, grad_proj, (((0,), (0,)), ((), ())), preferred_element_type=jnp.float32
    )
    all_nodes = nodes.shape[0] * lax.axis_size("row") * lax.axis_size("col")
    grad_weight = lax.psum(partial_grad, ("row", "col")) * (1.0 / math.sqrt(all_nodes))
    return (activated, grad_nodes, grad_weight)


def solution(mesh):
    return jax.shard_map(
        local,
        mesh=mesh,
        in_specs=(
            P(("row", "col"), None),
            P(),
            P("row", "col"),
            P(("row", "col"), None),
            P(("row", "col"), None),
            P(("row", "col")),
            P(("row", "col")),
            P(("row", "col"), None, None),
            P(("row", "col"), None),
        ),
        out_specs=(P(("row", "col"), None), P(("row", "col"), None), P()),
        check_vma=False,
    )
```

profile of v0, /device:TPU:1, one launch (start us, length us, event | category | flops | bytes accessed | tf_op | source)
XLA Modules:
  0.0 462.5 jit_solution(4636149198428322566)
XLA Ops:
  7.2 0.7 all-gather.6.cloned.1.call-update
  8.0 1.8 convolution_convert_fusion.2
  9.8 0.0 reduce-scatter.3.cloned.1.call-start
  9.8 0.7 compare_select_fusion
  10.5 54.9 %all-gather.6.cloned.1.call-done = bf16[128,128,256]{2,1,0:T(8,128)(2,1)} async-done(((bf16[8,128,256]{2,1,0:T(8,128)(2,1)}), bf16[128,128,256]{2,1,0:T(8,128)(2,1)}) %all-gather.6.cloned.1.call-update) | async-done | bytes 8388624 | tf_op jit(solution)/shard_map/all_gather | solution.py:18
  65.5 4.1 gather_fusion
  69.6 0.8 convolution_bitcast_fusion.1
  70.3 3.9 fusion.1
  74.3 28.5 %all-gather.4.cloned.1.call-done = bf16[4096,256]{1,0:T(8,128)(2,1)} async-done(((bf16[256,256]{1,0:T(8,128)(2,1)}), bf16[4096,256]{1,0:T(8,128)(2,1)}) %all-gather.4.cloned.1.call-update) | async-done | bytes 2097168 | tf_op jit(solution)/shard_map/all_gather | solution.py:15
  102.8 12.5 %fusion.4 = bf16[2048,256]{0,1:T(8,128)(2,1)} fusion(bf16[4096,256]{1,0:T(8,128)(2,1)} %all-gather.4.cloned.1.call-done, bf16[2048,4096]{1,0:T(8,128)(2,1)} %param.11, f32[32,8,16,128]{3,2,1,0:T(8,128)S(1)} %bitcast.38), kind=kOutput, calls=%fused_computation.7 | convolution fusion | flops 4296015872 | bytes 22020096 | tf_op jit(solution)/shard_map/dot_general | solution.py:28
  115.3 0.0 all-gather.8.cloned.1.call-start
  115.4 0.1 copy.17
  115.5 69.4 %reduce-scatter.3.cloned.1.call-done = bf16[256,256]{0,1:T(8,128)(2,1)} async-done(((bf16[2048,256]{0,1:T(8,128)(2,1)}), bf16[256,256]{0,1:T(8,128)(2,1)}) %reduce-scatter.3.cloned.1.call-update) | async-done | bytes 131088 | tf_op jit(solution)/shard_map/reduce_scatter | solution.py:29
  184.9 1.7 fusion.11
  186.6 0.2 reduce-scatter.5.cloned.1.call-start
  186.8 46.5 %all-gather.8.cloned.1.call-done = bf16[2048,256]{0,1:T(8,128)(2,1)} async-done(((bf16[256,256]{0,1:T(8,128)(2,1)}), bf16[2048,256]{0,1:T(8,128)(2,1)}) %all-gather.8.cloned.1.call-update) | async-done | bytes 1048592 | tf_op jit(solution)/shard_map/all_gather | solution.py:37
  233.3 11.9 %fusion = bf16[4096,256]{0,1:T(8,128)(2,1)} fusion(bf16[2048,256]{0,1:T(8,128)(2,1)} %all-gather.8.cloned.1.call-done, bf16[2048,4096]{1,0:T(8,128)(2,1)} %param.11), kind=kOutput, calls=%fused_computation.2 | convolution fusion | flops 4296015872 | bytes 19922944 | tf_op jit(solution)/shard_map/dot_general | solution.py:39
  245.3 0.8 copy.18
  246.1 58.0 %reduce-scatter.5.cloned.1.call-done = bf16[256,256]{0,1:T(8,128)(2,1)} async-done(((bf16[4096,256]{0,1:T(8,128)(2,1)}), bf16[256,256]{0,1:T(8,128)(2,1)}) %reduce-scatter.5.cloned.1.call-update) | async-done | bytes 131088 | tf_op jit(solution)/shard_map/reduce_scatter | solution.py:38
  304.1 1.8 convolution_bitcast_fusion.2
  305.9 1.8 convolution_convert_fusion.1
  307.7 146.1 %all-reduce.2.cloned.1.call-done = f32[256,256]{0,1:T(8,128)} async-done(((f32[256,256]{0,1:T(8,128)}), f32[256,256]{0,1:T(8,128)}) %all-reduce.2.cloned.1.call-update) | async-done | bytes 262160 | tf_op jit(solution)/shard_map/psum | solution.py:53
  453.8 1.0 broadcast_multiply_fusion
  454.8 0.8 copy.19
  (19 shorter events, 0.2 us)
Async XLA Ops:
  7.2 62.4 %copy-start = (bf16[32,128,128]{2,1,0:T(8,128)(2,1)S(1)}, bf16[32,128,128]{2,1,0:T(8,128)(2,1)}, u32[]{:S(2)}) copy-start(bf16[32,128,128]{2,1,0:T(8,128)(2,1)} %param.16) | copy-start | bytes 3145732
  7.2 58.3 %all-gather.6.cloned.1.call-start = ((), (), s32[]{:S(2)}) async-start(), calls=%async_computation.3 | async-start | bytes 8912896 | tf_op jit(solution)/shard_map/all_gather | solution.py:18
  7.9 94.9 %all-gather.4.cloned.1.call-start = ((), (), s32[]{:S(2)}) async-start(), calls=%async_computation.2 | async-start | bytes 2228224 | tf_op jit(solution)/shard_map/all_gather | solution.py:15
  9.8 175.1 %reduce-scatter.3.cloned.1.call-start = ((), (), s32[]{:S(2)}) async-start(), calls=%async_computation.4 | async-start | bytes 1179648 | tf_op jit(solution)/shard_map/reduce_scatter | solution.py:29
  69.6 0.8 copy-start.4
  102.8 12.6 %copy-start.3 = (bf16[256,256]{1,0:T(8,128)(2,1)S(1)}, bf16[256,256]{1,0:T(8,128)(2,1)}, u32[]{:S(2)}) copy-start(bf16[256,256]{1,0:T(8,128)(2,1)} %param.17) | copy-start | bytes 393220
  115.3 118.0 %all-gather.8.cloned.1.call-start = ((), (), s32[]{:S(2)}) async-start(), calls=%async_computation.5 | async-start | bytes 1179648 | tf_op jit(solution)/shard_map/all_gather | solution.py:37
  186.6 117.4 %reduce-scatter.5.cloned.1.call-start = ((), (), s32[]{:S(2)}) async-start(), calls=%async_computation.6 | async-start | bytes 2228224 | tf_op jit(solution)/shard_map/reduce_scatter | solution.py:38
  245.2 58.8 %copy-start.2 = (bf16[256,256]{1,0:T(8,128)(2,1)S(1)}, bf16[256,256]{1,0:T(8,128)(2,1)}, u32[]{:S(2)}) copy-start(bf16[256,256]{1,0:T(8,128)(2,1)} %param.9) | copy-start | bytes 393220
  245.2 60.6 %copy-start.1 = (bf16[256,256]{1,0:T(8,128)(2,1)S(1)}, bf16[256,256]{1,0:T(8,128)(2,1)}, u32[]{:S(2)}) copy-start(bf16[256,256]{1,0:T(8,128)(2,1)} %param.10) | copy-start | bytes 393220
  245.3 208.5 %all-reduce.2.cloned.1.call-start = ((), (), s32[]{:S(2)}) async-start(), calls=%async_computation.7 | async-start | bytes 524288 | tf_op jit(solution)/shard_map/psum | solution.py:53
Sparse Core Ops, SparseCore 0:
  9.7 55.7 all-gather.5
  67.7 34.9 all-gather.3
  115.4 69.4 reduce-scatter.2
  187.7 45.5 all-gather.7
  245.4 58.6 reduce-scatter.4
  310.0 143.8 all-reduce.1
where the time goes:
time: 463 us; the launch traced here: 462 us
  waiting for transfers between devices  404 us (87%)
  matrix products  34.5 us (7%)
  between operations  14.2 us (3%)
  local copies, waits for them, and re-layouts  5.78 us (1%)
    psum x1, waiting for transfers between devices, local(): lax.psum(partial_grad, ('row', 'col')) * (1.0 / math.sqrt(all_nodes))  146 us
    reduce_scatter x1, waiting for transfers between devices, local(): lax.psum_scatter((in_batch + history_term).astype(jnp.bfloat16), 'col', s...  69.4 us
    reduce_scatter x1, waiting for transfers between devices, local(): lax.psum_scatter(lax.dot_general(adjacency, grad_panel, (((0,), (0,)), ((...  58 us
    all_gather x1, waiting for transfers between devices, local(): everything = lax.all_gather(blocks, 'row', axis=0, tiled=True)  54.9 us
    all_gather x1, waiting for transfers between devices, local(): grad_panel = lax.all_gather(grad_pre, 'col', axis=0, tiled=True)  46.5 us
    all_gather x1, waiting for transfers between devices, local(): gathered = lax.all_gather(projected, 'row', axis=0, tiled=True)  28.5 us
    dot_general x1, matrix products, local(): in_batch = jnp.dot(adjacency, gathered, preferred_element_type=jnp.float32)  12.5 us
    dot_general x1, matrix products, local(): lax.dot_general(adjacency, grad_panel, (((0,), (0,)), ((), ())), preferre...  11.9 us
  transfers between devices with their start and end apart: 6, of which 6 were waited for; matrix products, arithmetic and copies ran while one was open for 3% of the time, Pallas kernels for 0%

commit v1 on v0

--- a/solution.py
+++ b/solution.py
@@ -50,7 +50,12 @@
         nodes, grad_proj, (((0,), (0,)), ((), ())), preferred_element_type=jnp.float32
     )
     all_nodes = nodes.shape[0] * lax.axis_size("row") * lax.axis_size("col")
-    grad_weight = lax.psum(partial_grad, ("row", "col")) * (1.0 / math.sqrt(all_nodes))
+
+    def kinds_direct(field):
+        carry = jax.lax.all_gather(field, ("row", "col")).sum(axis=0)
+        return carry
+
+    grad_weight = kinds_direct(partial_grad) * (1.0 / math.sqrt(all_nodes))
     return (activated, grad_nodes, grad_weight)
 
 

time: 463 us -> 689 us (1.49)
  waiting for transfers between devices: 404 us -> 608 us
  local copies, waits for them, and re-layouts: 5.78 us -> 25.4 us
    all_gather x0 -> x1, waiting for transfers between devices: none -> 349 us  [kinds_direct(): carry = jax.lax.all_gather(field, ('row', 'col')).sum(axis=0)]
    psum x1 -> x0, waiting for transfers between devices: 146 us -> none  [local(): lax.psum(partial_grad, ('row', 'col')) * (1.0 / math.sqrt(all_nodes))]
    unnamed x13 -> x16, local copies, waits for them, and re-layouts: 1.72 us -> 21.3 us
  transfers between devices with their start and end apart: 6 -> 6, of which waited for: 6 -> 6; matrix products, arithmetic and copies ran while one was open for 3% -> 2% of each run, Pallas kernels for 0% -> 0%
where the time goes in v1:
time: 689 us
  waiting for transfers between devices  608 us (88%)
  matrix products  34.5 us (5%)
  local copies, waits for them, and re-layouts  25.4 us (4%)
  between operations  14.2 us (2%)
    all_gather x1, waiting for transfers between devices, kinds_direct(): carry = jax.lax.all_gather(field, ('row', 'col')).sum(axis=0)  349 us
    reduce_scatter x1, waiting for transfers between devices, local(): lax.psum_scatter((in_batch + history_term).astype(jnp.bfloat16), 'col', s...  69.5 us
    reduce_scatter x1, waiting for transfers between devices, local(): lax.psum_scatter(lax.dot_general(adjacency, grad_panel, (((0,), (0,)), ((...  58.7 us
    all_gather x1, waiting for transfers between devices, local(): everything = lax.all_gather(blocks, 'row', axis=0, tiled=True)  54.9 us
    all_gather x1, waiting for transfers between devices, local(): grad_panel = lax.all_gather(grad_pre, 'col', axis=0, tiled=True)  46.4 us
    all_gather x1, waiting for transfers between devices, local(): gathered = lax.all_gather(projected, 'row', axis=0, tiled=True)  28.5 us
    unnamed x16, local copies, waits for them, and re-layouts  21.3 us
  transfers between devices with their start and end apart: 6, of which 6 were waited for; matrix products, arithmetic and copies ran while one was open for 2% of the time, Pallas kernels for 0%

profile of v1, /device:TPU:1, one launch (start us, length us, event | category | flops | bytes accessed | tf_op | source)
XLA Modules:
  0.0 689.0 jit_solution(17232893076609915504)
XLA Ops:
  7.2 0.7 all-gather.8.cloned.1.call-update
  8.0 1.8 convolution_convert_fusion.2
  9.8 0.7 compare_select_fusion
  10.5 54.9 %all-gather.8.cloned.1.call-done = bf16[128,128,256]{2,1,0:T(8,128)(2,1)} async-done(((bf16[8,128,256]{2,1,0:T(8,128)(2,1)}), bf16[128,128,256]{2,1,0:T(8,128)(2,1)}) %all-gather.8.cloned.1.call-update) | async-done | bytes 8388624 | tf_op jit(solution)/shard_map/all_gather | solution.py:18
  65.5 4.1 gather_fusion
  69.6 0.8 convolution_bitcast_fusion.1
  70.3 3.9 fusion.1
  74.3 28.5 %all-gather.6.cloned.1.call-done = bf16[4096,256]{1,0:T(8,128)(2,1)} async-done(((bf16[256,256]{1,0:T(8,128)(2,1)}), bf16[4096,256]{1,0:T(8,128)(2,1)}) %all-gather.6.cloned.1.call-update) | async-done | bytes 2097168 | tf_op jit(solution)/shard_map/all_gather | solution.py:15
  102.8 12.5 %fusion.4 = bf16[2048,256]{0,1:T(8,128)(2,1)} fusion(bf16[4096,256]{1,0:T(8,128)(2,1)} %all-gather.6.cloned.1.call-done, bf16[2048,4096]{1,0:T(8,128)(2,1)} %param.11, f32[32,8,16,128]{3,2,1,0:T(8,128)S(1)} %bitcast.44), kind=kOutput, calls=%fused_computation.8 | convolution fusion | flops 4296015872 | bytes 22020096 | tf_op jit(solution)/shard_map/dot_general | solution.py:28
  115.4 0.1 copy.16
  115.5 69.5 %reduce-scatter.3.cloned.1.call-done = bf16[256,256]{0,1:T(8,128)(2,1)} async-done(((bf16[2048,256]{0,1:T(8,128)(2,1)}), bf16[256,256]{0,1:T(8,128)(2,1)}) %reduce-scatter.3.cloned.1.call-update) | async-done | bytes 131088 | tf_op jit(solution)/shard_map/reduce_scatter | solution.py:29
  185.0 1.7 fusion.11
  186.7 0.2 reduce-scatter.5.cloned.1.call-start
  186.9 46.4 %all-gather.10.cloned.1.call-done = bf16[2048,256]{0,1:T(8,128)(2,1)} async-done(((bf16[256,256]{0,1:T(8,128)(2,1)}), bf16[2048,256]{0,1:T(8,128)(2,1)}) %all-gather.10.cloned.1.call-update) | async-done | bytes 1048592 | tf_op jit(solution)/shard_map/all_gather | solution.py:37
  233.3 11.9 %fusion = bf16[4096,256]{0,1:T(8,128)(2,1)} fusion(bf16[2048,256]{0,1:T(8,128)(2,1)} %all-gather.10.cloned.1.call-done, bf16[2048,4096]{1,0:T(8,128)(2,1)} %param.11), kind=kOutput, calls=%fused_computation.3 | convolution fusion | flops 4296015872 | bytes 19922944 | tf_op jit(solution)/shard_map/dot_general | solution.py:39
  245.2 0.0 all-gather.12.cloned.1.call-start
  245.3 58.7 %reduce-scatter.5.cloned.1.call-done = bf16[256,256]{0,1:T(8,128)(2,1)} async-done(((bf16[4096,256]{0,1:T(8,128)(2,1)}), bf16[256,256]{0,1:T(8,128)(2,1)}) %reduce-scatter.5.cloned.1.call-update) | async-done | bytes 131088 | tf_op jit(solution)/shard_map/reduce_scatter | solution.py:38
  304.0 1.8 convolution_bitcast_fusion.2
  305.9 0.8 copy.17
  306.6 1.8 convolution_convert_fusion.1
  308.4 349.1 %all-gather.12.cloned.1.call-done = f32[32768,256]{0,1:T(8,128)} async-done(((f32[256,256]{0,1:T(8,128)}), f32[32768,256]{0,1:T(8,128)}) %all-gather.12.cloned.1.call-update) | async-done | bytes 33554448 | tf_op jit(solution)/shard_map/all_gather | solution.py:55
  657.5 19.6 %copy.24 = f32[32,8,128,256]{3,2,1,0:T(8,128)S(1)} copy(f32[32,8,128,256]{3,1,2,0:T(8,128)} %bitcast.43) | data formatting | bytes 67108864
  677.1 4.1 bitcast_reduce_fusion
  681.3 0.8 copy.18
  (23 shorter events, 0.3 us)
Async XLA Ops:
  7.2 62.4 %copy-start = (bf16[32,128,128]{2,1,0:T(8,128)(2,1)S(1)}, bf16[32,128,128]{2,1,0:T(8,128)(2,1)}, u32[]{:S(2)}) copy-start(bf16[32,128,128]{2,1,0:T(8,128)(2,1)} %param.16) | copy-start | bytes 3145732
  7.2 58.3 %all-gather.8.cloned.1.call-start = ((), (), s32[]{:S(2)}) async-start(), calls=%async_computation.3 | async-start | bytes 8912896 | tf_op jit(solution)/shard_map/all_gather | solution.py:18
  7.9 94.9 %all-gather.6.cloned.1.call-start = ((), (), s32[]{:S(2)}) async-start(), calls=%async_computation.2 | async-start | bytes 2228224 | tf_op jit(solution)/shard_map/all_gather | solution.py:15
  9.8 175.2 %reduce-scatter.3.cloned.1.call-start = ((), (), s32[]{:S(2)}) async-start(), calls=%async_computation.4 | async-start | bytes 1179648 | tf_op jit(solution)/shard_map/reduce_scatter | solution.py:29
  69.6 0.8 copy-start.5
  102.8 12.6 %copy-start.4 = (bf16[256,256]{1,0:T(8,128)(2,1)S(1)}, bf16[256,256]{1,0:T(8,128)(2,1)}, u32[]{:S(2)}) copy-start(bf16[256,256]{1,0:T(8,128)(2,1)} %param.17) | copy-start | bytes 393220
  115.3 118.0 %all-gather.10.cloned.1.call-start = ((), (), s32[]{:S(2)}) async-start(), calls=%async_computation.5 | async-start | bytes 1179648 | tf_op jit(solution)/shard_map/all_gather | solution.py:37
  186.7 117.4 %copy-start.3 = (bf16[256,256]{1,0:T(8,128)(2,1)S(1)}, bf16[256,256]{1,0:T(8,128)(2,1)}, u32[]{:S(2)}) copy-start(bf16[256,256]{1,0:T(8,128)(2,1)} %param.9) | copy-start | bytes 393220
  186.7 119.9 %copy-start.2 = (bf16[256,256]{1,0:T(8,128)(2,1)S(1)}, bf16[256,256]{1,0:T(8,128)(2,1)}, u32[]{:S(2)}) copy-start(bf16[256,256]{1,0:T(8,128)(2,1)} %param.10) | copy-start | bytes 393220
  186.7 117.3 %reduce-scatter.5.cloned.1.call-start = ((), (), s32[]{:S(2)}) async-start(), calls=%async_computation.6 | async-start | bytes 2228224 | tf_op jit(solution)/shard_map/reduce_scatter | solution.py:38
  245.2 412.3 %all-gather.12.cloned.1.call-start = ((), (), s32[]{:S(2)}) async-start(), calls=%async_computation.7 | async-start | bytes 33816576 | tf_op jit(solution)/shard_map/all_gather | solution.py:55
  677.1 5.0 copy-start.1
Sparse Core Ops, SparseCore 0:
  9.7 55.7 all-gather.7
  67.8 34.9 all-gather.5
  115.4 69.5 reduce-scatter.2
  187.8 45.4 all-gather.9
  245.4 58.6 reduce-scatter.4
  306.3 351.2 all-gather.11
